TPU v7x, 32 devices: a whole 2x2x4 slice. The times are simulated.
32 devices in a mesh: fsdp: 4 (over x, core), ctx: 8 (over z, y).
Axes of the slice: x: 2, y: 2, z: 4, core: 2. Of those that a mesh axis runs over, the one named last changes fastest.
Arguments:
- hidden_in: bfloat16 [4, 1024, 576], P('fsdp', 'ctx'), may hold values from -6 to 6
- positions: int32 [4, 1024], P('fsdp', 'ctx'), may hold values from 0 to 1023, as said below
- block_pairs: int32 [4, 8], P('fsdp'), may hold values from 0 to 7, as said below
- norm_gains: bfloat16 [2, 576], P(None, 'ctx'), may hold values from 0.5 to 1.5
- w_query: bfloat16 [576, 576], P('fsdp', 'ctx'), may hold values from -0.25 to 0.25
- w_kv: bfloat16 [576, 384], P('fsdp', 'ctx'), may hold values from -0.25 to 0.25
- w_out: bfloat16 [576, 576], P('fsdp', 'ctx'), may hold values from -4 to 4
- w_gate_up: bfloat16 [576, 3072], P('fsdp', 'ctx'), may hold values from -0.25 to 0.25
- w_down: bfloat16 [1536, 576], P('fsdp', 'ctx'), may hold values from -0.15625 to 0.15625
- output_grad: bfloat16 [4, 1024, 576], P('fsdp', 'ctx'), may hold values from -6 to 6
Outputs:
- hidden_out: bfloat16 [4, 1024, 576], P('fsdp', 'ctx')
- input_grad: float32 [4, 1024, 576], P('fsdp', 'ctx')
- w_query_grad: float32 [576, 576], P('fsdp', 'ctx')
- w_kv_grad: float32 [576, 384], P('fsdp', 'ctx')
- w_out_grad: float32 [576, 576], P('fsdp', 'ctx')
- w_gate_up_grad: float32 [576, 3072], P('fsdp', 'ctx')
- w_down_grad: float32 [1536, 576], P('fsdp', 'ctx')
- gains_grad: float32 [2, 576], P(None, 'ctx')
Inputs may be any that keep to these rules, and one draw needn't show every extreme that they name: Each row is a permutation of 0 to 7; context device c holds blocks block_pairs[s, c] and 15 - block_pairs[s, c] of 64 tokens of sequence s, in that order. `positions`: A row's position counts tokens from the start of its document; documents are packed into each sequence in order, sequence 0 is a single document, and rows stand in the dealt order of block_pairs.
All inputs are finite; a program needn't handle non-finite values.
Results may differ from a plain program's by a relative error of at most 0.013.
Values may be sent and summed in bfloat16 or wider, within the bound.
A program may use at most 128 MiB of HBM per device.

v0:
```python
import functools
import math

import jax
import jax.numpy as jnp
from jax import lax
from jax.experimental import pallas as pl
from jax.experimental.pallas import tpu as pltpu
from jax.sharding import PartitionSpec as P

H = 9
KVH = 3
HD = 64
FF = 1536


EPSILON = 1e-05
THETA = 100000.0

MESH_ID = pl.DeviceIdType.MESH
PAIR = 2


def greet(peers):
    barrier = pltpu.get_barrier_semaphore()
    for peer in peers:
        pl.semaphore_signal(barrier, inc=1, device_id=peer, device_id_type=MESH_ID)
    pl.semaphore_wait(barrier, len(peers))


class Place:
    def __init__(self, fsdp, ctx):
        self.nk, self.nx = PAIR, fsdp // PAIR
        self.ny, self.nz = PAIR, ctx // PAIR
        f = lax.axis_index("fsdp")
        c = lax.axis_index("ctx")
        self.f, self.c = f, c
        self.x, self.k = f // self.nk, f % self.nk
        self.z, self.y = c // self.ny, c % self.ny

    def rel(self, dx=0, dk=0, dz=0, dy=0):
        fx = (self.x + dx) % self.nx if dx else self.x
        fk = (self.k + dk) % self.nk if dk else self.k
        cz = (self.z + dz) % self.nz if dz else self.z
        cy = (self.y + dy) % self.ny if dy else self.y
        return (fx * self.nk + fk, cz * self.ny + cy)

    def peers(self):
        return (
            [self.rel(dx=d) for d in range(1, self.nx)]
            + [self.rel(dk=d) for d in range(1, self.nk)]
            + [self.rel(dz=d) for d in range(1, self.nz)]
            + [self.rel(dy=d) for d in range(1, self.ny)]
        )


def gather_kernel(fsdp, ctx, w_ref, h_ref, wout, hout, wsend, wrecv, hsend, hrecv, own_sem):
    me = Place(fsdp, ctx)
    nx, nk, nz, ny = me.nx, me.nk, me.nz, me.ny
    own_w = pltpu.make_async_copy(w_ref, wout.at[me.f, me.c], own_sem.at[0])
    own_h = pltpu.make_async_copy(h_ref, hout.at[me.c], own_sem.at[1])
    own_w.start()
    own_h.start()
    greet(me.peers())
    sends = []

    def push_w(kx, kk, kz, ky, stage, step, src=None):
        f, c = me.rel(dx=kx, dk=kk, dz=kz, dy=ky)
        offs = {stage: step}
        dest = me.rel(**offs)
        new = dict(dx=kx, dk=kk, dz=kz, dy=ky)
        size = dict(dx=nx, dk=nk, dz=nz, dy=ny)[stage]
        new[stage] = (new[stage] - step) % size
        slot = ((new["dx"] * nk + new["dk"]) * nz + new["dz"]) * ny + new["dy"]
        copy = pltpu.make_async_remote_copy(
            src_ref=wout.at[f, c] if src is None else src,
            dst_ref=wout.at[f, c],
            send_sem=wsend.at[slot],
            recv_sem=wrecv.at[slot],
            device_id=dest,
            device_id_type=MESH_ID,
        )
        copy.start()
        sends.append(copy)

    def wait_w(kx, kk, kz, ky):
        f, c = me.rel(dx=kx, dk=kk, dz=kz, dy=ky)
        slot = ((kx * nk + kk) * nz + kz) * ny + ky
        pltpu.make_async_remote_copy(
            src_ref=wout.at[f, c],
            dst_ref=wout.at[f, c],
            send_sem=wsend.at[slot],
            recv_sem=wrecv.at[slot],
            device_id=me.rel(dk=1),
            device_id_type=MESH_ID,
        ).wait_recv()

    def push_h(kz, ky, stage, step, src=None):
        c = me.rel(dz=kz, dy=ky)[1]
        dest = me.rel(**{stage: step})
        new = dict(dz=kz, dy=ky)
        new[stage] = (new[stage] - step) % dict(dz=nz, dy=ny)[stage]
        slot = new["dz"] * ny + new["dy"]
        copy = pltpu.make_async_remote_copy(
            src_ref=hout.at[c] if src is None else src,
            dst_ref=hout.at[c],
            send_sem=hsend.at[slot],
            recv_sem=hrecv.at[slot],
            device_id=dest,
            device_id_type=MESH_ID,
        )
        copy.start()
        sends.append(copy)

    def wait_h(kz, ky):
        c = me.rel(dz=kz, dy=ky)[1]
        slot = kz * ny + ky
        pltpu.make_async_remote_copy(
            src_ref=hout.at[c],
            dst_ref=hout.at[c],
            send_sem=hsend.at[slot],
            recv_sem=hrecv.at[slot],
            device_id=me.rel(dk=1),
            device_id_type=MESH_ID,
        ).wait_recv()

    for d in range(1, nx):
        push_w(0, 0, 0, 0, "dx", d, w_ref)
    for d in range(1, nz):
        push_w(0, 0, 0, 0, "dz", d, w_ref)
    for d in range(1, ny):
        push_w(0, 0, 0, 0, "dy", d, w_ref)
    for d in range(1, nk):
        push_w(0, 0, 0, 0, "dk", d, w_ref)
    for d in range(1, nz):
        push_h(0, 0, "dz", d, h_ref)
    for d in range(1, ny):
        push_h(0, 0, "dy", d, h_ref)
    for kz in range(1, nz):
        wait_w(0, 0, kz, 0)
        for d in range(1, nx):
            push_w(0, 0, kz, 0, "dx", d)
        for d in range(1, ny):
            push_w(0, 0, kz, 0, "dy", d)
        for d in range(1, nk):
            push_w(0, 0, kz, 0, "dk", d)
    for ky in range(1, ny):
        for kz in range(nz):
            wait_w(0, 0, kz, ky)
            for d in range(1, nx):
                push_w(0, 0, kz, ky, "dx", d)
            for d in range(1, nk):
                push_w(0, 0, kz, ky, "dk", d)
    for kz in range(1, nz):
        wait_h(kz, 0)
        for d in range(1, ny):
            push_h(kz, 0, "dy", d)
    for ky in range(1, ny):
        for kz in range(nz):
            wait_h(kz, ky)
    for kx in range(1, nx):
        for ky in range(ny):
            for kz in range(nz):
                wait_w(kx, 0, kz, ky)
                for d in range(1, nk):
                    push_w(kx, 0, kz, ky, "dk", d)
    for kk in range(1, nk):
        for kx in range(nx):
            for ky in range(ny):
                for kz in range(nz):
                    wait_w(kx, kk, kz, ky)
    for copy in sends:
        copy.wait_send()
    own_w.wait()
    own_h.wait()


def gather_all(packed, rows):
    fsdp, ctx = lax.axis_size("fsdp"), lax.axis_size("ctx")
    return pl.pallas_call(
        functools.partial(gather_kernel, fsdp, ctx),
        out_shape=(
            jax.ShapeDtypeStruct((fsdp, ctx) + packed.shape, packed.dtype),
            jax.ShapeDtypeStruct((ctx,) + rows.shape, rows.dtype),
        ),
        in_specs=[pl.BlockSpec(memory_space=pltpu.VMEM)] * 2,
        out_specs=[pl.BlockSpec(memory_space=pl.ANY)] * 2,
        scratch_shapes=[
            pltpu.SemaphoreType.DMA((fsdp * ctx,)),
            pltpu.SemaphoreType.DMA((fsdp * ctx,)),
            pltpu.SemaphoreType.DMA((ctx,)),
            pltpu.SemaphoreType.DMA((ctx,)),
            pltpu.SemaphoreType.DMA((2,)),
        ],
        compiler_params=pltpu.CompilerParams(collective_id=0, has_side_effects=True),
    )(packed, rows)


def exchange_kernel(fsdp, ctx, part_ref, out_ref, held_y, held_z, send, recv_y, recv_z):
    me = Place(fsdp, ctx)
    nz, ny = me.nz, me.ny
    greet(
        [me.rel(dz=d) for d in range(1, nz)] + [me.rel(dy=d) for d in range(1, ny)],
    )
    sends = []
    y_copies, z_copies = {}, {}
    order_z = list(range(1, nz)) + [0]
    for dz in order_z:
        for dy in range(1, ny):
            slot = (dy - 1) * nz + dz
            copy = pltpu.make_async_remote_copy(
                src_ref=part_ref.at[me.rel(dz=dz, dy=dy)[1]],
                dst_ref=held_y.at[slot],
                send_sem=send.at[len(sends)],
                recv_sem=recv_y.at[slot],
                device_id=me.rel(dy=dy),
                device_id_type=MESH_ID,
            )
            copy.start()
            sends.append(copy)
            y_copies[dz, dy] = copy

    def y_sum(dz):
        total = part_ref[me.rel(dz=dz)[1]].astype(jnp.float32)
        for dy in range(1, ny):
            y_copies[dz, dy].wait_recv()
            total = total + held_y[(dy - 1) * nz + dz].astype(jnp.float32)
        return total

    for dz in range(1, nz):
        held_y[dz] = y_sum(dz).astype(held_y.dtype)
        copy = pltpu.make_async_remote_copy(
            src_ref=held_y.at[dz],
            dst_ref=held_z.at[dz - 1],
            send_sem=send.at[len(sends)],
            recv_sem=recv_z.at[dz - 1],
            device_id=me.rel(dz=dz),
            device_id_type=MESH_ID,
        )
        copy.start()
        sends.append(copy)
        z_copies[dz] = copy
    total = y_sum(0)
    for dz in range(1, nz):
        z_copies[dz].wait_recv()
        total = total + held_z[dz - 1].astype(jnp.float32)
    out_ref[...] = total
    for copy in sends:
        copy.wait_send()


def exchange_sum(parts):
    fsdp, ctx = lax.axis_size("fsdp"), lax.axis_size("ctx")
    counts = ((PAIR - 1) * (ctx // PAIR), ctx // PAIR - 1)
    return pl.pallas_call(
        functools.partial(exchange_kernel, fsdp, ctx),
        out_shape=jax.ShapeDtypeStruct(parts.shape[1:], jnp.float32),
        in_specs=[pl.BlockSpec(memory_space=pltpu.VMEM)],
        out_specs=pl.BlockSpec(memory_space=pltpu.VMEM),
        scratch_shapes=[pltpu.VMEM((n,) + parts.shape[1:], parts.dtype) for n in counts]
        + [pltpu.SemaphoreType.DMA((n,)) for n in (sum(counts),) + counts],
        compiler_params=pltpu.CompilerParams(
            collective_id=1, has_side_effects=True, vmem_limit_bytes=48 * 2**20
        ),
    )(parts)


def scatter_kernel(
    fsdp, ctx, g_ref, out_ref, held_k, held_x, held_y, held_z, send, recv_k, recv_x, recv_y, recv_z
):
    me = Place(fsdp, ctx)
    nx, nz, ny = me.nx, me.nz, me.ny
    greet(me.peers())
    sends = []

    def push(src, dst, dst_sem, dest):
        copy = pltpu.make_async_remote_copy(
            src_ref=src,
            dst_ref=dst,
            send_sem=send.at[len(sends)],
            recv_sem=dst_sem,
            device_id=dest,
            device_id_type=MESH_ID,
        )
        copy.start()
        sends.append(copy)

    def wait(ref, sem):
        pltpu.make_async_remote_copy(
            src_ref=ref,
            dst_ref=ref,
            send_sem=sem,
            recv_sem=sem,
            device_id=me.rel(dk=1),
            device_id_type=MESH_ID,
        ).wait_recv()

    order_x = list(range(1, nx)) + [0]
    order_c = [(dy, dz) for dy in list(range(1, ny)) + [0] for dz in list(range(1, nz)) + [0]]
    for dx in order_x:
        for dy, dz in order_c:
            f, c = me.rel(dx=dx, dk=1, dz=dz, dy=dy)
            slot = (dx * nz + dz) * ny + dy
            push(g_ref.at[f, c], held_k.at[slot], recv_k.at[slot], me.rel(dk=1))

    def local_sum(dx, dz, dy):
        f, c = me.rel(dx=dx, dz=dz, dy=dy)
        slot = (dx * nz + dz) * ny + dy
        wait(held_k.at[slot], recv_k.at[slot])
        return g_ref[f, c].astype(jnp.float32) + held_k[slot].astype(jnp.float32), slot

    for dx in order_x[:-1]:
        for dy, dz in order_c:
            total, slot = local_sum(dx, dz, dy)
            held_k[slot] = total.astype(held_k.dtype)
            there = ((dx - 1) * nz + dz) * ny + dy
            push(held_k.at[slot], held_x.at[there], recv_x.at[there], me.rel(dx=dx))

    def x_sum(dz, dy):
        total, slot = local_sum(0, dz, dy)
        for dx in range(1, nx):
            there = ((dx - 1) * nz + dz) * ny + dy
            wait(held_x.at[there], recv_x.at[there])
            total = total + held_x[there].astype(jnp.float32)
        return total, slot

    for dy in range(1, ny):
        for dz in list(range(1, nz)) + [0]:
            total, slot = x_sum(dz, dy)
            held_k[slot] = total.astype(held_k.dtype)
            there = (dy - 1) * nz + dz
            push(held_k.at[slot], held_y.at[there], recv_y.at[there], me.rel(dy=dy))

    def y_sum(dz):
        total, slot = x_sum(dz, 0)
        for dy in range(1, ny):
            there = (dy - 1) * nz + dz
            wait(held_y.at[there], recv_y.at[there])
            total = total + held_y[there].astype(jnp.float32)
        return total, slot

    for dz in range(1, nz):
        total, slot = y_sum(dz)
        held_k[slot] = total.astype(held_k.dtype)
        push(held_k.at[slot], held_z.at[dz - 1], recv_z.at[dz - 1], me.rel(dz=dz))
    total, slot = y_sum(0)
    for dz in range(1, nz):
        wait(held_z.at[dz - 1], recv_z.at[dz - 1])
        total = total + held_z[dz - 1].astype(jnp.float32)
    out_ref[...] = total
    for copy in sends:
        copy.wait_send()


def scatter_sum(grads):
    fsdp, ctx, rows, lanes = grads.shape
    nx, nz, ny = fsdp // PAIR, ctx // PAIR, PAIR
    counts = (nx * ctx, (nx - 1) * ctx, (ny - 1) * nz, nz - 1)
    return pl.pallas_call(
        functools.partial(scatter_kernel, fsdp, ctx),
        out_shape=jax.ShapeDtypeStruct((rows, lanes), jnp.float32),
        in_specs=[pl.BlockSpec(memory_space=pltpu.VMEM)],
        out_specs=pl.BlockSpec(memory_space=pltpu.VMEM),
        scratch_shapes=[pltpu.VMEM((n, rows, lanes), grads.dtype) for n in counts]
        + [pltpu.SemaphoreType.DMA((n,)) for n in (sum(counts),) + counts],
        compiler_params=pltpu.CompilerParams(
            collective_id=2, has_side_effects=True, vmem_limit_bytes=48 * 2**20
        ),
    )(grads)


def unfold(pieces, row_count, col_count):
    fsdp, ctx = pieces.shape[:2]
    shaped = pieces.reshape(fsdp, ctx, row_count, col_count)
    return shaped.transpose(0, 2, 1, 3).reshape(fsdp * row_count, ctx * col_count)


def fold(whole, fsdp, ctx):
    row_count, col_count = whole.shape
    shaped = whole.reshape(fsdp, row_count // fsdp, ctx, col_count // ctx)
    return shaped.transpose(0, 2, 1, 3)


def block_times(pair_row, block_len, ctx_count):
    within_ids = jnp.arange(2 * block_len, dtype=jnp.int32)[None, :]
    first_block = pair_row[:, None]
    block_ids = jnp.where(within_ids < block_len, first_block, 2 * ctx_count - 1 - first_block)
    return (block_ids * block_len + within_ids % block_len).reshape(-1)


def rope_tables(token_pos, head_size):
    half_size = head_size // 2
    freq_vec = THETA ** (-(jnp.arange(half_size, dtype=jnp.float32) * 2.0) / head_size)
    angles = token_pos.astype(jnp.float32)[:, None] * freq_vec[None, :]
    cos_half = jnp.cos(angles)
    sin_half = jnp.sin(angles)
    return (jnp.concatenate([cos_half, cos_half], 1), jnp.concatenate([sin_half, sin_half], 1))


def rotate(values, cos_table, sin_table, head_count):
    row_count = values.shape[0]
    shaped = values.reshape(row_count, head_count, -1)
    half_size = shaped.shape[2] // 2
    turned = jnp.concatenate([-shaped[:, :, half_size:], shaped[:, :, :half_size]], 2)
    return (shaped * cos_table[:, None, :] + turned * sin_table[:, None, :]).reshape(row_count, -1)


def rotate_back(grad_vals, cos_table, sin_table, head_count):
    row_count = grad_vals.shape[0]
    shaped = grad_vals.reshape(row_count, head_count, -1)
    half_size = shaped.shape[2] // 2
    scaled = shaped * sin_table[:, None, :]
    turned = jnp.concatenate([scaled[:, :, half_size:], -scaled[:, :, :half_size]], 2)
    return (shaped * cos_table[:, None, :] + turned).reshape(row_count, -1)


def norm_forward(values, gain_vec):
    inv_scale = lax.rsqrt(jnp.mean(values * values, axis=1, keepdims=True) + EPSILON)
    return (values * inv_scale * gain_vec[None, :], inv_scale)


def norm_backward(values, inv_scale, gain_vec, grad_out):
    weighted = grad_out * gain_vec[None, :]
    gain_grad = jnp.sum(grad_out * values * inv_scale, axis=0)
    inner_mean = jnp.mean(weighted * values, axis=1, keepdims=True)
    return (inv_scale * weighted - values * inv_scale**3 * inner_mean, gain_grad)


def score_block(query_grp, key_blk, query_time, key_time):
    scores = jnp.einsum(
        "qkgd,skd->kgqs", query_grp, key_blk, preferred_element_type=jnp.float32
    ) * HD ** (-0.5)
    key_mask = key_time[None, None, None, :] <= query_time[None, None, :, None]
    return (scores, key_mask)


def attend(query_b, kv_all, query_time, key_time):
    tok_count = query_b.shape[0]
    length = kv_all.shape[0]
    width = math.gcd(length, 1024)
    block_count = length // width
    group_size = H // KVH
    query_grp = query_b.reshape(tok_count, KVH, group_size, HD)
    kv_blocks = kv_all.reshape(block_count, width, 2, KVH, HD)
    time_blocks = key_time.reshape(block_count, width)

    def total_step(running, block_in):
        kv_blk, time_blk = block_in
        scores, key_mask = score_block(query_grp, kv_blk[:, 0], query_time, time_blk)
        return (running + jnp.sum(jnp.where(key_mask, jnp.exp(scores), 0.0), axis=3), None)

    totals = lax.scan(
        total_step, jnp.zeros((KVH, group_size, tok_count), jnp.float32), (kv_blocks, time_blocks)
    )[0]
    logsum = jnp.log(totals)

    def output_step(running, block_in):
        kv_blk, time_blk = block_in
        scores, key_mask = score_block(query_grp, kv_blk[:, 0], query_time, time_blk)
        prob_b = jnp.where(key_mask, jnp.exp(scores - logsum[:, :, :, None]), 0.0).astype(
            jnp.bfloat16
        )
        part_out = jnp.einsum(
            "kgqs,skd->qkgd", prob_b, kv_blk[:, 1], preferred_element_type=jnp.float32
        )
        return (running + part_out, None)

    attn_out = lax.scan(
        output_step,
        jnp.zeros((tok_count, KVH, group_size, HD), jnp.float32),
        (kv_blocks, time_blocks),
    )[0]
    return (attn_out.reshape(tok_count, -1).astype(jnp.bfloat16), logsum)


def attend_back(query_b, kv_all, query_time, key_time, logsum, attn_b, attn_grad_b):
    tok_count = query_b.shape[0]
    length = kv_all.shape[0]
    width = math.gcd(length, 1024)
    block_count = length // width
    group_size = H // KVH
    query_grp = query_b.reshape(tok_count, KVH, group_size, HD)
    grad_grp = attn_grad_b.reshape(tok_count, KVH, group_size, HD)
    product = attn_grad_b.astype(jnp.float32) * attn_b.astype(jnp.float32)
    delta_sum = jnp.sum(product.reshape(tok_count, KVH, group_size, HD), axis=3).transpose(1, 2, 0)
    kv_blocks = kv_all.reshape(block_count, width, 2, KVH, HD)
    time_blocks = key_time.reshape(block_count, width)

    def back_step(running, block_in):
        kv_blk, time_blk = block_in
        scores, key_mask = score_block(query_grp, kv_blk[:, 0], query_time, time_blk)
        prob_f = jnp.where(key_mask, jnp.exp(scores - logsum[:, :, :, None]), 0.0)
        prob_grad = jnp.einsum(
            "qkgd,skd->kgqs", grad_grp, kv_blk[:, 1], preferred_element_type=jnp.float32
        )
        score_grad = (prob_f * (prob_grad - delta_sum[:, :, :, None]) * HD ** (-0.5)).astype(
            jnp.bfloat16
        )
        query_next = running + jnp.einsum(
            "kgqs,skd->qkgd", score_grad, kv_blk[:, 0], preferred_element_type=jnp.float32
        )
        key_grad = jnp.einsum(
            "kgqs,qkgd->skd", score_grad, query_grp, preferred_element_type=jnp.float32
        )
        value_grad = jnp.einsum(
            "kgqs,qkgd->skd",
            prob_f.astype(jnp.bfloat16),
            grad_grp,
            preferred_element_type=jnp.float32,
        )
        return (
            query_next,
            jnp.concatenate([key_grad.reshape(width, -1), value_grad.reshape(width, -1)], 1),
        )

    query_grad, kv_grad = lax.scan(
        back_step,
        jnp.zeros((tok_count, KVH, group_size, HD), jnp.float32),
        (kv_blocks, time_blocks),
    )
    return (query_grad.reshape(tok_count, -1), kv_grad.reshape(length, -1))


def body(
    hidden_in,
    positions,
    block_pairs,
    norm_gains,
    w_query,
    w_kv,
    w_out,
    w_gate_up,
    w_down,
    output_grad,
):
    tok_count = hidden_in.shape[1]
    ctx_count = lax.axis_size("ctx")
    block_len = tok_count // 2
    kv_dim = KVH * HD
    grad_scale = 1.0 / math.sqrt(lax.axis_size("fsdp") * ctx_count * tok_count)
    fsdp_count = lax.axis_size("fsdp")
    width = hidden_in.shape[2]
    row_d, col_q = w_query.shape
    col_k, col_o, col_g = w_kv.shape[1], w_out.shape[1], w_gate_up.shape[1]
    lanes, col_d = w_down.shape
    small = jnp.concatenate([w_query.T, w_kv.T, w_out.T], 0)
    gain_flat = norm_gains.reshape(-1)
    n_gu = row_d * col_g // lanes
    n_small = small.size // lanes
    n_gain = -(-gain_flat.size // lanes)
    cut_down, cut_small = n_gu + col_d, n_gu + col_d + n_small
    n_rows = -(-(cut_small + n_gain) // 16) * 16
    gain_rows = jnp.pad(gain_flat, (0, (n_rows - cut_small) * lanes - gain_flat.size))
    packed = jnp.concatenate(
        [
            w_gate_up.reshape(n_gu, lanes),
            w_down.T,
            small.reshape(n_small, lanes),
            gain_rows.reshape(-1, lanes),
        ],
        0,
    )
    pos_cols = jnp.stack([positions[0] // 128, positions[0] % 128], 1).astype(jnp.bfloat16)
    spare = (-(width + 2)) % 128
    rows_b = jnp.concatenate([hidden_in[0], jnp.pad(pos_cols, ((0, 0), (0, spare)))], 1)
    gathered, rows_all = gather_all(packed, rows_b)
    wgu_full = unfold(gathered[:, :, :n_gu], row_d, col_g)
    wdown_t = gathered[:, :, n_gu:cut_down].transpose(1, 2, 0, 3).reshape(ctx_count * col_d, -1)
    col_s = small.shape[0]
    small_all = gathered[:, :, cut_down:cut_small].reshape(fsdp_count, ctx_count, col_s, row_d)
    small_all = small_all.transpose(1, 2, 0, 3).reshape(ctx_count, col_s, fsdp_count * row_d)
    wq_t = small_all[:, :col_q].reshape(ctx_count * col_q, -1)
    wkv_t = small_all[:, col_q : col_q + col_k].reshape(ctx_count * col_k, -1)
    wo_t = small_all[:, col_q + col_k :].reshape(ctx_count * col_o, -1)
    gain_all = gathered[0, :, cut_small:].reshape(ctx_count, -1)[:, : gain_flat.size]
    gain_all = gain_all.reshape(ctx_count, 2, -1).transpose(1, 0, 2).reshape(2, -1)
    gain_one = gain_all[0].astype(jnp.float32)
    gain_two = gain_all[1].astype(jnp.float32)
    rows_in = hidden_in[0].astype(jnp.float32)
    normed_one, scale_one = norm_forward(rows_in, gain_one)
    normed_one_b = normed_one.astype(jnp.bfloat16)
    query = jnp.einsum("td,qd->tq", normed_one_b, wq_t, preferred_element_type=jnp.float32)
    cos_table, sin_table = rope_tables(positions[0], HD)
    query_b = rotate(query, cos_table, sin_table, H).astype(jnp.bfloat16)
    rows_all = rows_all.reshape(ctx_count * tok_count, -1)
    normed_all = norm_forward(rows_all[:, :width].astype(jnp.float32), gain_one)[0]
    kv_proj = jnp.einsum(
        "td,kd->tk", normed_all.astype(jnp.bfloat16), wkv_t, preferred_element_type=jnp.float32
    )
    pos_all = rows_all[:, width : width + 2].astype(jnp.float32)
    cos_all, sin_all = rope_tables(pos_all[:, 0] * 128.0 + pos_all[:, 1], HD)
    key_b = rotate(kv_proj[:, :kv_dim], cos_all, sin_all, KVH).astype(jnp.bfloat16)
    kv_all = jnp.concatenate([key_b, kv_proj[:, kv_dim:].astype(jnp.bfloat16)], 1)
    key_time = block_times(block_pairs[0], block_len, ctx_count)
    query_time = lax.dynamic_slice_in_dim(key_time, lax.axis_index("ctx") * tok_count, tok_count)
    attn_b, logsum = attend(query_b, kv_all, query_time, key_time)
    mixed = rows_in + jnp.einsum("tq,dq->td", attn_b, wo_t, preferred_element_type=jnp.float32)
    normed_two, scale_two = norm_forward(mixed, gain_two)
    normed_two_b = normed_two.astype(jnp.bfloat16)
    gate_up = jnp.dot(normed_two_b, wgu_full, preferred_element_type=jnp.float32)
    gate_part = gate_up[:, :FF]
    up_part = gate_up[:, FF:]
    sig_gate = jax.nn.sigmoid(gate_part)
    silu_gate = gate_part * sig_gate
    act_b = (silu_gate * up_part).astype(jnp.bfloat16)
    down_out = jnp.einsum("tf,df->td", act_b, wdown_t, preferred_element_type=jnp.float32)
    result = (mixed + down_out).astype(jnp.bfloat16)
    grad_b = output_grad[0]
    act_grad = jnp.einsum("td,df->tf", grad_b, wdown_t, preferred_element_type=jnp.float32)
    wdown_grad_t = jnp.einsum("td,tf->df", grad_b, act_b, preferred_element_type=jnp.float32)
    gate_grad = act_grad * up_part * sig_gate * (1.0 + gate_part * (1.0 - sig_gate))
    gu_grad_b = jnp.concatenate([gate_grad, act_grad * silu_gate], 1).astype(jnp.bfloat16)
    wgu_grad = jnp.einsum("td,tf->df", normed_two_b, gu_grad_b, preferred_element_type=jnp.float32)
    normed_two_grad = jnp.einsum(
        "tf,df->td", gu_grad_b, wgu_full, preferred_element_type=jnp.float32
    )
    mixed_back, gain_term_two = norm_backward(mixed, scale_two, gain_two, normed_two_grad)
    mixed_grad = grad_b.astype(jnp.float32) + mixed_back
    mixed_grad_b = mixed_grad.astype(jnp.bfloat16)
    wo_grad_t = jnp.einsum("td,tq->dq", mixed_grad_b, attn_b, preferred_element_type=jnp.float32)
    attn_grad_b = jnp.einsum(
        "td,dq->tq", mixed_grad_b, wo_t, preferred_element_type=jnp.float32
    ).astype(jnp.bfloat16)
    query_grad, kv_terms = attend_back(
        query_b, kv_all, query_time, key_time, logsum, attn_b, attn_grad_b
    )
    kv_grad = exchange_sum(
        kv_terms.reshape(ctx_count, tok_count, 2 * kv_dim).astype(jnp.bfloat16)
    )
    query_pre = rotate_back(query_grad, cos_table, sin_table, H).astype(jnp.bfloat16)
    key_pre = rotate_back(kv_grad[:, :kv_dim], cos_table, sin_table, KVH)
    kv_pre = jnp.concatenate([key_pre, kv_grad[:, kv_dim:]], 1).astype(jnp.bfloat16)
    wq_grad_t = jnp.einsum("tq,td->qd", query_pre, normed_one_b, preferred_element_type=jnp.float32)
    wkv_grad_t = jnp.einsum("tk,td->kd", kv_pre, normed_one_b, preferred_element_type=jnp.float32)
    normed_one_grad = jnp.einsum(
        "tq,qd->td", query_pre, wq_t, preferred_element_type=jnp.float32
    ) + jnp.einsum("tk,kd->td", kv_pre, wkv_t, preferred_element_type=jnp.float32)
    rows_back, gain_term_one = norm_backward(rows_in, scale_one, gain_one, normed_one_grad)
    input_grad = mixed_grad + rows_back
    small_grads = jnp.concatenate(
        [
            g.astype(jnp.bfloat16).reshape(ctx_count, -1, fsdp_count * row_d)
            for g in (wq_grad_t, wkv_grad_t, wo_grad_t)
        ],
        1,
    )
    small_grads = small_grads.reshape(ctx_count, col_s, fsdp_count, row_d).transpose(2, 0, 1, 3)
    gain_grads = jnp.stack([gain_term_one, gain_term_two]).reshape(2, ctx_count, -1)
    gain_grads = gain_grads.transpose(1, 0, 2).reshape(ctx_count, -1).astype(jnp.bfloat16)
    gain_pad = (n_rows - cut_small) * lanes - gain_flat.size
    gain_grads = jnp.pad(gain_grads, ((0, 0), (0, gain_pad))).reshape(1, ctx_count, -1, lanes)
    down_pieces = wdown_grad_t.astype(jnp.bfloat16).reshape(ctx_count, col_d, fsdp_count, lanes)
    pieces = jnp.concatenate(
        [
            fold(wgu_grad.astype(jnp.bfloat16), fsdp_count, ctx_count).reshape(
                fsdp_count, ctx_count, n_gu, lanes
            ),
            down_pieces.transpose(2, 0, 1, 3),
            small_grads.reshape(fsdp_count, ctx_count, n_small, lanes),
            jnp.broadcast_to(gain_grads, (fsdp_count,) + gain_grads.shape[1:]),
        ],
        2,
    )
    owned = scatter_sum(pieces) * grad_scale
    small_owned = owned[cut_down:cut_small].reshape(-1, row_d).T
    owned_grads = (
        small_owned[:, :col_q],
        small_owned[:, col_q : col_q + col_k],
        small_owned[:, col_q + col_k :],
        owned[:n_gu].reshape(row_d, col_g),
        owned[n_gu:cut_down].T,
    )
    gains_owned = owned[cut_small:].reshape(-1)[: gain_flat.size].reshape(2, -1)
    return (
        result[None],
        input_grad[None],
        owned_grads[0],
        owned_grads[1],
        owned_grads[2],
        owned_grads[3],
        owned_grads[4],
        gains_owned,
    )


def solution(mesh):
    return jax.shard_map(
        body,
        mesh=mesh,
        in_specs=(
            P("fsdp", "ctx", None),
            P("fsdp", "ctx"),
            P("fsdp", None),
            P(None, "ctx"),
            P("fsdp", "ctx"),
            P("fsdp", "ctx"),
            P("fsdp", "ctx"),
            P("fsdp", "ctx"),
            P("fsdp", "ctx"),
            P("fsdp", "ctx", None),
        ),
        out_specs=(
            P("fsdp", "ctx", None),
            P("fsdp", "ctx", None),
            P("fsdp", "ctx"),
            P("fsdp", "ctx"),
            P("fsdp", "ctx"),
            P("fsdp", "ctx"),
            P("fsdp", "ctx"),
            P(None, "ctx"),
        ),
        check_vma=False,
    )
```

profile of v0, /device:TPU:0, one launch (start us, length us, event | category | flops | bytes accessed | tf_op | source)
XLA Modules:
  0.0 266.6 jit_solution(12046683740994855470)
XLA Ops:
  0.7 0.7 reshape.477
  5.1 0.9 copy.173
  6.0 0.9 pad_maximum_fusion.11
  7.2 0.7 copy.195
  8.0 0.9 broadcast_compare_fusion
  8.8 1.1 copy.172
  10.5 0.7 fusion.54.h_ref
  11.3 1.7 copy.186
  13.0 1.6 pad_maximum_fusion.8.w_ref
  14.6 59.0 %shard_map.161 = (bf16[4,8,304,384]{3,2,1,0:T(8,128)(2,1)}, bf16[8,128,640]{2,1,0:T(8,128)(2,1)}) custom-call(bf16[304,384]{1,0:T(8,128)(2,1)} %pad_maximum_fusion.8.w_ref, bf16[128,640]{1,0:T(8,128)(2,1)} %fusion.54.h_ref), custom_call_target="tpu_custom_call" | custom-call | tf_op jit(solution)/shard_map/pallas_call | solution.py:180
  73.7 1.7 fusion.12
  75.3 0.9 slice_bitcast_fusion.14
  76.5 1.1 slice.170
  78.3 0.9 pad_maximum_fusion.6
  79.2 2.4 slice_bitcast_fusion
  81.6 2.4 slice_bitcast_fusion.1
  84.0 1.4 copy.184
  85.3 1.6 copy.232
  86.9 0.8 copy.183
  87.7 2.6 copy.231
  90.3 6.5 %reshape.481 = bf16[4,8,192,144]{3,2,1,0:T(8,128)(2,1)} reshape(bf16[4,8,72,384]{3,2,1,0:T(8,128)(2,1)S(1)} %get-tuple-element.128) | data formatting | bytes 3538944 | tf_op jit(solution)/shard_map/reshape | solution.py:570
  96.7 3.4 %copy.176 = bf16[8,192,4,144]{1,3,2,0:T(8,128)(2,1)S(1)} copy(bf16[8,192,4,144]{3,1,0,2:T(8,128)(2,1)} %bitcast.226) | data formatting | bytes 3538944 | tf_op jit(solution)/shard_map/transpose | solution.py:571
  100.5 1.3 copy.177
  101.8 1.6 fusion.77
  103.5 2.3 copy.181
  105.7 2.3 fusion.18
  108.0 0.8 slice.244
  108.9 0.8 copy.179
  109.7 1.6 fusion.60
  111.3 0.8 fusion.52
  112.4 0.8 copy-done.21
  113.4 0.9 copy-done.11
  114.3 4.4 %fusion.2 = f32[3,3,128,1024]{2,3,1,0:T(8,128)} fusion(pred[128,1024]{0,1:T(8,128)(4,1)S(1)} %copy-done.32, bf16[128,3,3,64]{0,3,2,1:T(8,128)(2,1)S(1)} %bitcast.257, bf16[1024,2,3,64]{0,3,2,1:T(8,128)(2,1)S(1)} %bitcast.236), kind=kOutput, calls=%fused_computation.4 | convolution fusion | flops 307890304 | bytes 6062080 | tf_op jit(solution)/shard_map/while/body/eval_jaxpr/reduce_sum | solution.py:450
  118.7 3.1 %fusion.28 = bf16[3,64,3,128]{3,1,2,0:T(8,128)(2,1)S(1)} fusion(f32[3,3,128,1024]{2,3,1,0:T(8,128)} %fusion.2, bf16[1024,2,3,64]{0,3,2,1:T(8,128)(2,1)} %bitcast.237), kind=kOutput, calls=%fused_computation.46 | convolution fusion | flops 152248320 | bytes 5259264 | tf_op jit(solution)/shard_map/while/body/eval_jaxpr/kgqs,skd->qkgd/dot_general | solution.py:463
  122.9 0.8 fusion.76
  124.4 1.6 multiply_convert_fusion.1
  126.0 0.7 copy-done.17
  126.8 1.4 fusion.32
  128.2 1.7 copy.209
  129.9 3.9 %multiply_reduce_fusion = (bf16[576]{0:T(1024)(128)(2,1)}, f32[128]{0:T(128)}, f32[128,576]{1,0:T(8,128)}) fusion(f32[128,576]{1,0:T(8,128)} %copy-done.1, f32[128]{0:T(128)S(1)} %get-tuple-element.153, f32[576]{0:T(1024)S(1)} %reshape.499, bf16[576,3072]{1,0:T(8,128)(2,1)S(1)} %bitcast.223, bf16[128,1536]{1,0:T(8,128)(2,1)} %get-tuple-element.130, ...), kind=kOutput, calls=%fused_computation.84 | convolution fusion | flops 454999360 | bytes 4919680 | tf_op jit(solution)/shard_map/tf,df->td/dot_general | solution.py:614
  133.7 0.8 stack.17
  135.2 1.3 subtract_add_fusion
  136.4 1.6 convert_multiply_fusion.7
  138.0 3.3 %fusion.23 = bf16[3,64,1024]{2,1,0:T(8,128)(2,1)S(1)} fusion(bf16[128,3,3,64]{0,3,2,1:T(8,128)(2,1)S(1)} %bitcast.254, f32[3,3,128,1024]{2,3,1,0:T(8,128)} %fusion.2), kind=kOutput, calls=%fused_computation.38 | convolution fusion | flops 152371200 | bytes 5259264 | tf_op jit(solution)/shard_map/while/body/eval_jaxpr/kgqs,qkgd->skd/dot_general | solution.py:505
  141.3 3.2 %fusion.5 = bf16[3,3,128,1024]{2,3,1,0:T(8,128)(2,1)S(1)} fusion(f32[3,3,128,1024]{2,3,1,0:T(8,128)} %fusion.2, f32[3,3,128]{2,1,0:T(4,128)S(1)} %bitcast.271, bf16[128,3,3,64]{0,3,2,1:T(8,128)(2,1)S(1)} %bitcast.255, bf16[1024,2,3,64]{0,3,2,1:T(8,128)(2,1)S(1)} %bitcast.238), kind=kOutput, calls=%fused_computation.8 | convolution fusion | flops 155713536 | bytes 7624704 | tf_op jit(solution)/shard_map/while/body/eval_jaxpr/qkgd,skd->kgqs/dot_general | solution.py:493
  145.5 0.9 fusion.22
  147.4 30.0 %shard_map.162 = f32[128,384]{1,0:T(8,128)S(1)} custom-call(bf16[8,128,384]{2,1,0:T(8,128)(2,1)S(1)} %pad_maximum_fusion.3.part_ref), custom_call_target="tpu_custom_call" | custom-call | tf_op jit(solution)/shard_map/pallas_call | solution.py:255
  179.3 0.9 copy.210
  181.3 0.8 broadcast_in_dim.126
  182.1 0.8 concatenate.91
  182.8 1.2 copy.205
  184.5 0.8 concatenate.89
  185.2 1.2 copy.203
  186.4 1.0 reshape.505
  187.4 1.5 copy.204
  189.0 2.1 maximum_bitcast_fusion
  191.1 5.5 %reshape.494 = bf16[4,8,72,384]{3,2,1,0:T(8,128)(2,1)} reshape(bf16[4,8,192,144]{3,2,1,0:T(8,128)(2,1)S(1)} %maximum_bitcast_fusion) | data formatting | bytes 3538944 | tf_op jit(solution)/shard_map/reshape | solution.py:659
  196.6 1.5 fusion.11
  199.8 1.2 convolution_convert_fusion
  201.0 0.8 copy.235
  202.4 1.0 copy-done.6
  203.4 3.5 %pad_maximum_fusion.g_ref = bf16[4,8,304,384]{3,2,1,0:T(8,128)(2,1)} fusion(bf16[4,8,16,384]{3,2,1,0:T(8,128)(2,1)S(1)} %copy-done.19, bf16[4,8,72,384]{3,2,1,0:T(8,128)(2,1)S(1)} %copy-done.6, bf16[4,8,72,384]{3,2,1,0:T(8,128)(2,1)S(1)} %bitcast.228, bf16[4,8,144,384]{3,2,1,0:T(8,128)(2,1)S(1)} %bitcast.221), kind=kLoop, calls=%fused_computation.1 | loop fusion | flops 29884416 | bytes 14942208 | tf_op jit(solution)/shard_map/concatenate | solution.py:653
  206.9 55.3 %shard_map.163 = f32[304,384]{1,0:T(8,128)S(1)} custom-call(bf16[4,8,304,384]{3,2,1,0:T(8,128)(2,1)} %pad_maximum_fusion.g_ref), custom_call_target="tpu_custom_call" | custom-call | tf_op jit(solution)/shard_map/pallas_call | solution.py:359
  265.1 0.7 copy.212
  (149 shorter events, 19.5 us)
Async XLA Ops:
  5.1 2.8 %copy-start.28 = (f32[128,64]{0,1:T(8,128)}, f32[128,64]{0,1:T(8,128)S(1)}, u32[]{:S(2)}) copy-start(f32[128,64]{0,1:T(8,128)S(1)} %get-tuple-element.162) | copy-start | bytes 98308
  9.9 69.3 %copy-start.3 = (bf16[1,128,576]{2,1,0:T(8,128)(2,1)}, bf16[1,128,576]{2,1,0:T(8,128)(2,1)S(1)}, u32[]{:S(2)}) copy-start(bf16[1,128,576]{2,1,0:T(8,128)(2,1)S(1)} %copy.172) | copy-start | bytes 442372
  109.7 2.6 copy-start.8
  109.7 2.6 copy-start.22
  112.1 1.2 copy-start.23
  112.1 1.0 copy-start.21
  112.2 1.1 copy-start.16
  112.3 2.0 copy-start.32
  113.4 0.9 copy-start.11
  118.7 3.1 %copy-start.4 = (bf16[1,128,576]{2,1,0:T(8,128)(2,1)S(1)}, bf16[1,128,576]{2,1,0:T(8,128)(2,1)}, u32[]{:S(2)}) copy-start(bf16[1,128,576]{2,1,0:T(8,128)(2,1)} %copy-done.3) | copy-start | bytes 442372
  118.7 3.1 %copy-start.10 = (bf16[8,72,576]{2,1,0:T(8,128)(2,1)S(1)}, bf16[8,72,576]{2,1,0:T(8,128)(2,1)}, u32[]{:S(2)}) copy-start(bf16[8,72,576]{2,1,0:T(8,128)(2,1)} %copy.181) | copy-start | bytes 1990660
  118.7 4.2 %copy-start = (bf16[72,8,8,384]{3,1,2,0:T(8,128)(2,1)S(1)}, bf16[72,8,8,384]{3,1,2,0:T(8,128)(2,1)}, u32[]{:S(2)}) copy-start(bf16[72,8,8,384]{3,1,2,0:T(8,128)(2,1)} %copy.231) | copy-start | bytes 10616836
  121.8 1.9 copy-start.13
  122.3 3.7 %copy-start.1 = (f32[128,576]{1,0:T(8,128)}, f32[128,576]{1,0:T(8,128)S(1)}, u32[]{:S(2)}) copy-start(f32[128,576]{1,0:T(8,128)S(1)} %get-tuple-element.157) | copy-start | bytes 884740
  122.9 1.5 copy-start.7
  122.9 1.5 copy-start.25
  126.0 0.8 copy-start.17
  138.0 3.3 %copy-start.12 = (bf16[1024,384]{0,1:T(8,128)(2,1)S(1)}, bf16[1024,384]{0,1:T(8,128)(2,1)}, u32[]{:S(2)}) copy-start(bf16[1024,384]{0,1:T(8,128)(2,1)} %copy-done.11) | copy-start | bytes 2359300
  144.6 0.9 copy-start.24
  146.5 31.2 %copy-start.27 = (f32[128,64]{0,1:T(8,128)S(1)}, f32[128,64]{0,1:T(8,128)}, u32[]{:S(2)}) copy-start(f32[128,64]{0,1:T(8,128)} %get-tuple-element.163) | copy-start | bytes 98308
  146.8 31.0 %copy-start.26 = (f32[128,192]{1,0:T(8,128)S(1)}, f32[128,192]{1,0:T(8,128)}, u32[]{:S(2)}) copy-start(f32[128,192]{1,0:T(8,128)} %copy.195) | copy-start | bytes 294916
  147.1 30.9 %copy-start.29 = (f32[128,64]{0,1:T(8,128)S(1)}, f32[128,64]{0,1:T(8,128)}, u32[]{:S(2)}) copy-start(f32[128,64]{0,1:T(8,128)} %copy-done.28) | copy-start | bytes 98308
  147.4 30.6 %copy-start.9 = (bf16[8,72,576]{2,1,0:T(8,128)(2,1)S(1)}, bf16[8,72,576]{2,1,0:T(8,128)(2,1)}, u32[]{:S(2)}) copy-start(bf16[8,72,576]{2,1,0:T(8,128)(2,1)} %copy-done.8) | copy-start | bytes 1990660
  177.4 0.9 copy-start.5
  177.4 1.1 copy-start.15
  177.8 1.4 copy-start.33
  178.0 2.7 copy-start.14
  181.3 2.8 %copy-start.20 = (bf16[1,128,576]{1,2,0:T(8,128)(2,1)S(1)}, bf16[1,128,576]{1,2,0:T(8,128)(2,1)}, u32[]{:S(2)}) copy-start(bf16[1,128,576]{1,2,0:T(8,128)(2,1)} %param.10) | copy-start | bytes 442372
  191.1 5.5 %copy-start.18 = (bf16[128,1536]{1,0:T(8,128)(2,1)S(1)}, bf16[128,1536]{1,0:T(8,128)(2,1)}, u32[]{:S(2)}) copy-start(bf16[128,1536]{1,0:T(8,128)(2,1)} %copy-done.17) | copy-start | bytes 1179652
  198.6 1.0 copy-start.2
  198.6 1.1 copy-start.30
  198.6 1.2 copy-start.31
  201.9 1.5 copy-start.6
  201.9 1.5 copy-start.19
where the time goes:
time: 268 us; the launch traced here: 267 us
  Pallas kernels  144 us (54%)
  local copies, waits for them, and re-layouts  65.3 us (24%)
  matrix products  33.7 us (13%)
  other arithmetic  21.4 us (8%)
    pallas_call x1, Pallas kernels, gather_all(): pl.pallas_call(functools.partial(gather_kernel, fsdp, ctx), out_shape=(ja...  59 us
    pallas_call x1, Pallas kernels, scatter_sum(): pl.pallas_call(functools.partial(scatter_kernel, fsdp, ctx), out_shape=ja...  55.3 us
    pallas_call x1, Pallas kernels, exchange_sum(): pl.pallas_call(functools.partial(exchange_kernel, fsdp, ctx), out_shape=j...  30 us
    unnamed x83, local copies, waits for them, and re-layouts  19.6 us
    reshape x1, local copies, waits for them, and re-layouts, body(): gathered[:, :, cut_down:cut_small]  6.46 us
    concatenate x6, local copies, waits for them, and re-layouts, body(): jnp.concatenate([g.astype(jnp.bfloat16).reshape(ctx_count, -1, fsdp_count...  6.43 us
    reshape x1, local copies, waits for them, and re-layouts, body(): small_grads.reshape(fsdp_count, ctx_count, n_small, lanes)  5.53 us

commit v1 on v0

--- a/solution.py
+++ b/solution.py
@@ -124,46 +124,58 @@
             device_id_type=MESH_ID,
         ).wait_recv()
 
+    if nz > 1:
+        push_w(0, 0, 0, 0, "dz", 1, w_ref)
     for d in range(1, nx):
         push_w(0, 0, 0, 0, "dx", d, w_ref)
-    for d in range(1, nz):
-        push_w(0, 0, 0, 0, "dz", d, w_ref)
     for d in range(1, ny):
         push_w(0, 0, 0, 0, "dy", d, w_ref)
     for d in range(1, nk):
         push_w(0, 0, 0, 0, "dk", d, w_ref)
-    for d in range(1, nz):
-        push_h(0, 0, "dz", d, h_ref)
+    if nz > 1:
+        push_h(0, 0, "dz", 1, h_ref)
     for d in range(1, ny):
         push_h(0, 0, "dy", d, h_ref)
-    for kz in range(1, nz):
+    for kz in range(nz - 1, 0, -1):
         wait_w(0, 0, kz, 0)
+        if kz > 1:
+            push_w(0, 0, kz, 0, "dz", 1)
         for d in range(1, nx):
             push_w(0, 0, kz, 0, "dx", d)
         for d in range(1, ny):
             push_w(0, 0, kz, 0, "dy", d)
         for d in range(1, nk):
             push_w(0, 0, kz, 0, "dk", d)
-    for ky in range(1, ny):
-        for kz in range(nz):
-            wait_w(0, 0, kz, ky)
+        for ky in range(1, ny):
+            before = (kz + 1) % nz
+            wait_w(0, 0, before, ky)
             for d in range(1, nx):
-                push_w(0, 0, kz, ky, "dx", d)
+                push_w(0, 0, before, ky, "dx", d)
             for d in range(1, nk):
-                push_w(0, 0, kz, ky, "dk", d)
-    for kz in range(1, nz):
+                push_w(0, 0, before, ky, "dk", d)
         wait_h(kz, 0)
+        if kz > 1:
+            push_h(kz, 0, "dz", 1)
         for d in range(1, ny):
             push_h(kz, 0, "dy", d)
     for ky in range(1, ny):
+        last = 1 % nz
+        wait_w(0, 0, last, ky)
+        for d in range(1, nx):
+            push_w(0, 0, last, ky, "dx", d)
+        for d in range(1, nk):
+            push_w(0, 0, last, ky, "dk", d)
         for kz in range(nz):
             wait_h(kz, ky)
+    arrival = [(0, 0)]
+    for kz in range(nz - 1, 0, -1):
+        arrival += [(kz, 0)] + [((kz + 1) % nz, ky) for ky in range(1, ny)]
+    arrival += [(1 % nz, ky) for ky in range(1, ny)]
     for kx in range(1, nx):
-        for ky in range(ny):
-            for kz in range(nz):
-                wait_w(kx, 0, kz, ky)
-                for d in range(1, nk):
-                    push_w(kx, 0, kz, ky, "dk", d)
+        for kz, ky in arrival:
+            wait_w(kx, 0, kz, ky)
+            for d in range(1, nk):
+                push_w(kx, 0, kz, ky, "dk", d)
     for kk in range(1, nk):
         for kx in range(nx):
             for ky in range(ny):

time: 268 us -> 247 us (0.922)
  Pallas kernels: 144 us -> 123 us
    pallas_call x1, Pallas kernels: 30 us -> 16 us  [exchange_sum(): pl.pallas_call(functools.partial(exchange_kernel, fsdp, ctx), out_shape=j...]
    pallas_call x1, Pallas kernels: 59 us -> 52 us  [gather_all(): pl.pallas_call(functools.partial(gather_kernel, fsdp, ctx), out_shape=(ja...]
where the time goes in v1:
time: 247 us; the launch traced here: 245 us
  Pallas kernels  123 us (50%)
  local copies, waits for them, and re-layouts  65.3 us (26%)
  matrix products  33.7 us (14%)
  other arithmetic  21.4 us (9%)
    pallas_call x1, Pallas kernels, scatter_sum(): pl.pallas_call(functools.partial(scatter_kernel, fsdp, ctx), out_shape=ja...  55.3 us
    pallas_call x1, Pallas kernels, gather_all(): pl.pallas_call(functools.partial(gather_kernel, fsdp, ctx), out_shape=(ja...  52 us
    unnamed x83, local copies, waits for them, and re-layouts  19.6 us
    pallas_call x1, Pallas kernels, exchange_sum(): pl.pallas_call(functools.partial(exchange_kernel, fsdp, ctx), out_shape=j...  16 us
    reshape x1, local copies, waits for them, and re-layouts, body(): gathered[:, :, cut_down:cut_small]  6.46 us
    concatenate x6, local copies, waits for them, and re-layouts, body(): jnp.concatenate([g.astype(jnp.bfloat16).reshape(ctx_count, -1, fsdp_count...  6.43 us
    reshape x1, local copies, waits for them, and re-layouts, body(): small_grads.reshape(fsdp_count, ctx_count, n_small, lanes)  5.53 us

profile of v1, /device:TPU:0, one launch (start us, length us, event | category | flops | bytes accessed | tf_op | source)
XLA Modules:
  0.0 245.5 jit_solution(14437721501417132493)
XLA Ops:
  0.7 0.7 reshape.477
  5.1 0.9 copy.173
  6.0 0.9 pad_maximum_fusion.11
  7.2 0.7 copy.195
  8.0 0.9 broadcast_compare_fusion
  8.8 1.1 copy.172
  10.5 0.7 fusion.54.h_ref
  11.3 1.7 copy.186
  13.0 1.6 pad_maximum_fusion.8.w_ref
  14.6 52.0 %shard_map.161 = (bf16[4,8,304,384]{3,2,1,0:T(8,128)(2,1)}, bf16[8,128,640]{2,1,0:T(8,128)(2,1)}) custom-call(bf16[304,384]{1,0:T(8,128)(2,1)} %pad_maximum_fusion.8.w_ref, bf16[128,640]{1,0:T(8,128)(2,1)} %fusion.54.h_ref), custom_call_target="tpu_custom_call" | custom-call | tf_op jit(solution)/shard_map/pallas_call | solution.py:192
  66.7 1.7 fusion.12
  68.3 0.9 slice_bitcast_fusion.14
  69.5 1.1 slice.170
  71.3 0.9 pad_maximum_fusion.6
  72.2 2.4 slice_bitcast_fusion
  74.6 2.4 slice_bitcast_fusion.1
  77.0 1.4 copy.184
  78.3 1.6 copy.232
  79.9 0.8 copy.183
  80.7 2.6 %copy.231 = bf16[72,8,8,384]{3,1,2,0:T(8,128)(2,1)} copy(bf16[72,8,8,384]{3,2,1,0:T(8,128)(2,1)S(1)} %bitcast.224) | data formatting | bytes 7077888
  83.3 6.5 %reshape.481 = bf16[4,8,192,144]{3,2,1,0:T(8,128)(2,1)} reshape(bf16[4,8,72,384]{3,2,1,0:T(8,128)(2,1)S(1)} %get-tuple-element.128) | data formatting | bytes 3538944 | tf_op jit(solution)/shard_map/reshape | solution.py:582
  89.8 3.4 %copy.176 = bf16[8,192,4,144]{1,3,2,0:T(8,128)(2,1)S(1)} copy(bf16[8,192,4,144]{3,1,0,2:T(8,128)(2,1)} %bitcast.226) | data formatting | bytes 3538944 | tf_op jit(solution)/shard_map/transpose | solution.py:583
  93.5 1.3 copy.177
  94.8 1.6 fusion.77
  96.5 2.3 copy.181
  98.7 2.3 fusion.18
  101.1 0.8 slice.244
  101.9 0.8 copy.179
  102.7 1.6 fusion.60
  104.3 0.8 fusion.52
  105.4 0.8 copy-done.21
  106.4 0.9 copy-done.11
  107.3 4.4 %fusion.2 = f32[3,3,128,1024]{2,3,1,0:T(8,128)} fusion(pred[128,1024]{0,1:T(8,128)(4,1)S(1)} %copy-done.32, bf16[128,3,3,64]{0,3,2,1:T(8,128)(2,1)S(1)} %bitcast.257, bf16[1024,2,3,64]{0,3,2,1:T(8,128)(2,1)S(1)} %bitcast.236), kind=kOutput, calls=%fused_computation.4 | convolution fusion | flops 307890304 | bytes 6062080 | tf_op jit(solution)/shard_map/while/body/eval_jaxpr/reduce_sum | solution.py:462
  111.7 3.1 %fusion.28 = bf16[3,64,3,128]{3,1,2,0:T(8,128)(2,1)S(1)} fusion(f32[3,3,128,1024]{2,3,1,0:T(8,128)} %fusion.2, bf16[1024,2,3,64]{0,3,2,1:T(8,128)(2,1)} %bitcast.237), kind=kOutput, calls=%fused_computation.46 | convolution fusion | flops 152248320 | bytes 5259264 | tf_op jit(solution)/shard_map/while/body/eval_jaxpr/kgqs,skd->qkgd/dot_general | solution.py:475
  115.9 0.8 fusion.76
  117.4 1.6 multiply_convert_fusion.1
  119.0 0.7 copy-done.17
  119.8 1.4 fusion.32
  121.2 1.7 copy.209
  122.9 3.9 %multiply_reduce_fusion = (bf16[576]{0:T(1024)(128)(2,1)}, f32[128]{0:T(128)}, f32[128,576]{1,0:T(8,128)}) fusion(f32[128,576]{1,0:T(8,128)} %copy-done.1, f32[128]{0:T(128)S(1)} %get-tuple-element.153, f32[576]{0:T(1024)S(1)} %reshape.499, bf16[576,3072]{1,0:T(8,128)(2,1)S(1)} %bitcast.223, bf16[128,1536]{1,0:T(8,128)(2,1)} %get-tuple-element.130, ...), kind=kOutput, calls=%fused_computation.84 | convolution fusion | flops 454999360 | bytes 4919680 | tf_op jit(solution)/shard_map/tf,df->td/dot_general | solution.py:626
  126.7 0.8 stack.17
  128.2 1.3 subtract_add_fusion
  129.4 1.6 convert_multiply_fusion.7
  131.0 3.3 %fusion.23 = bf16[3,64,1024]{2,1,0:T(8,128)(2,1)S(1)} fusion(bf16[128,3,3,64]{0,3,2,1:T(8,128)(2,1)S(1)} %bitcast.254, f32[3,3,128,1024]{2,3,1,0:T(8,128)} %fusion.2), kind=kOutput, calls=%fused_computation.38 | convolution fusion | flops 152371200 | bytes 5259264 | tf_op jit(solution)/shard_map/while/body/eval_jaxpr/kgqs,qkgd->skd/dot_general | solution.py:517
  134.3 3.2 %fusion.5 = bf16[3,3,128,1024]{2,3,1,0:T(8,128)(2,1)S(1)} fusion(f32[3,3,128,1024]{2,3,1,0:T(8,128)} %fusion.2, f32[3,3,128]{2,1,0:T(4,128)S(1)} %bitcast.271, bf16[128,3,3,64]{0,3,2,1:T(8,128)(2,1)S(1)} %bitcast.255, bf16[1024,2,3,64]{0,3,2,1:T(8,128)(2,1)S(1)} %bitcast.238), kind=kOutput, calls=%fused_computation.8 | convolution fusion | flops 155713536 | bytes 7624704 | tf_op jit(solution)/shard_map/while/body/eval_jaxpr/qkgd,skd->kgqs/dot_general | solution.py:505
  138.5 0.9 fusion.22
  140.4 16.0 %shard_map.162 = f32[128,384]{1,0:T(8,128)S(1)} custom-call(bf16[8,128,384]{2,1,0:T(8,128)(2,1)S(1)} %pad_maximum_fusion.3.part_ref), custom_call_target="tpu_custom_call" | custom-call | tf_op jit(solution)/shard_map/pallas_call | solution.py:267
  158.3 0.9 copy.210
  160.3 0.8 broadcast_in_dim.126
  161.0 0.8 concatenate.91
  161.8 1.2 copy.205
  163.4 0.8 concatenate.89
  164.2 1.2 copy.203
  165.4 1.0 reshape.505
  166.4 1.5 copy.204
  167.9 2.1 maximum_bitcast_fusion
  170.1 5.5 %reshape.494 = bf16[4,8,72,384]{3,2,1,0:T(8,128)(2,1)} reshape(bf16[4,8,192,144]{3,2,1,0:T(8,128)(2,1)S(1)} %maximum_bitcast_fusion) | data formatting | bytes 3538944 | tf_op jit(solution)/shard_map/reshape | solution.py:671
  175.6 1.5 fusion.11
  178.8 1.2 convolution_convert_fusion
  180.0 0.8 copy.235
  181.3 1.0 copy-done.6
  182.4 3.5 %pad_maximum_fusion.g_ref = bf16[4,8,304,384]{3,2,1,0:T(8,128)(2,1)} fusion(bf16[4,8,16,384]{3,2,1,0:T(8,128)(2,1)S(1)} %copy-done.19, bf16[4,8,72,384]{3,2,1,0:T(8,128)(2,1)S(1)} %copy-done.6, bf16[4,8,72,384]{3,2,1,0:T(8,128)(2,1)S(1)} %bitcast.228, bf16[4,8,144,384]{3,2,1,0:T(8,128)(2,1)S(1)} %bitcast.221), kind=kLoop, calls=%fused_computation.1 | loop fusion | flops 29884416 | bytes 14942208 | tf_op jit(solution)/shard_map/concatenate | solution.py:665
  185.9 55.3 %shard_map.163 = f32[304,384]{1,0:T(8,128)S(1)} custom-call(bf16[4,8,304,384]{3,2,1,0:T(8,128)(2,1)} %pad_maximum_fusion.g_ref), custom_call_target="tpu_custom_call" | custom-call | tf_op jit(solution)/shard_map/pallas_call | solution.py:371
  244.0 0.7 copy.212
  (149 shorter events, 19.5 us)
Async XLA Ops:
  5.1 2.8 %copy-start.28 = (f32[128,64]{0,1:T(8,128)}, f32[128,64]{0,1:T(8,128)S(1)}, u32[]{:S(2)}) copy-start(f32[128,64]{0,1:T(8,128)S(1)} %get-tuple-element.162) | copy-start | bytes 98308
  9.9 62.3 %copy-start.3 = (bf16[1,128,576]{2,1,0:T(8,128)(2,1)}, bf16[1,128,576]{2,1,0:T(8,128)(2,1)S(1)}, u32[]{:S(2)}) copy-start(bf16[1,128,576]{2,1,0:T(8,128)(2,1)S(1)} %copy.172) | copy-start | bytes 442372
  102.7 2.6 %copy-start.8 = (bf16[8,72,576]{2,1,0:T(8,128)(2,1)}, bf16[8,72,576]{2,1,0:T(8,128)(2,1)S(1)}, u32[]{:S(2)}) copy-start(bf16[8,72,576]{2,1,0:T(8,128)(2,1)S(1)} %copy.179) | copy-start | bytes 1990660
  102.7 2.6 %copy-start.22 = (f32[1024,64]{0,1:T(8,128)S(1)}, f32[1024,64]{0,1:T(8,128)}, u32[]{:S(2)}) copy-start(f32[1024,64]{0,1:T(8,128)} %get-tuple-element.165) | copy-start | bytes 786436
  105.1 1.2 copy-start.23
  105.1 1.0 copy-start.21
  105.2 1.1 copy-start.16
  105.3 2.0 copy-start.32
  106.4 0.9 copy-start.11
  111.7 3.1 %copy-start.4 = (bf16[1,128,576]{2,1,0:T(8,128)(2,1)S(1)}, bf16[1,128,576]{2,1,0:T(8,128)(2,1)}, u32[]{:S(2)}) copy-start(bf16[1,128,576]{2,1,0:T(8,128)(2,1)} %copy-done.3) | copy-start | bytes 442372
  111.7 3.1 %copy-start.10 = (bf16[8,72,576]{2,1,0:T(8,128)(2,1)S(1)}, bf16[8,72,576]{2,1,0:T(8,128)(2,1)}, u32[]{:S(2)}) copy-start(bf16[8,72,576]{2,1,0:T(8,128)(2,1)} %copy.181) | copy-start | bytes 1990660
  111.7 4.2 %copy-start = (bf16[72,8,8,384]{3,1,2,0:T(8,128)(2,1)S(1)}, bf16[72,8,8,384]{3,1,2,0:T(8,128)(2,1)}, u32[]{:S(2)}) copy-start(bf16[72,8,8,384]{3,1,2,0:T(8,128)(2,1)} %copy.231) | copy-start | bytes 10616836
  114.8 1.9 copy-start.13
  115.3 3.7 %copy-start.1 = (f32[128,576]{1,0:T(8,128)}, f32[128,576]{1,0:T(8,128)S(1)}, u32[]{:S(2)}) copy-start(f32[128,576]{1,0:T(8,128)S(1)} %get-tuple-element.157) | copy-start | bytes 884740
  115.9 1.5 copy-start.7
  115.9 1.5 copy-start.25
  119.0 0.8 copy-start.17
  131.0 3.3 %copy-start.12 = (bf16[1024,384]{0,1:T(8,128)(2,1)S(1)}, bf16[1024,384]{0,1:T(8,128)(2,1)}, u32[]{:S(2)}) copy-start(bf16[1024,384]{0,1:T(8,128)(2,1)} %copy-done.11) | copy-start | bytes 2359300
  137.6 0.9 copy-start.24
  139.5 17.1 %copy-start.27 = (f32[128,64]{0,1:T(8,128)S(1)}, f32[128,64]{0,1:T(8,128)}, u32[]{:S(2)}) copy-start(f32[128,64]{0,1:T(8,128)} %get-tuple-element.163) | copy-start | bytes 98308
  139.8 17.0 %copy-start.26 = (f32[128,192]{1,0:T(8,128)S(1)}, f32[128,192]{1,0:T(8,128)}, u32[]{:S(2)}) copy-start(f32[128,192]{1,0:T(8,128)} %copy.195) | copy-start | bytes 294916
  140.1 16.8 %copy-start.29 = (f32[128,64]{0,1:T(8,128)S(1)}, f32[128,64]{0,1:T(8,128)}, u32[]{:S(2)}) copy-start(f32[128,64]{0,1:T(8,128)} %copy-done.28) | copy-start | bytes 98308
  140.4 16.6 %copy-start.9 = (bf16[8,72,576]{2,1,0:T(8,128)(2,1)S(1)}, bf16[8,72,576]{2,1,0:T(8,128)(2,1)}, u32[]{:S(2)}) copy-start(bf16[8,72,576]{2,1,0:T(8,128)(2,1)} %copy-done.8) | copy-start | bytes 1990660
  156.4 0.9 copy-start.5
  156.4 1.1 copy-start.15
  156.8 1.4 copy-start.33
  157.0 2.7 %copy-start.14 = (bf16[3,64,3,128]{3,1,2,0:T(8,128)(2,1)S(1)}, bf16[3,64,3,128]{3,1,2,0:T(8,128)(2,1)}, u32[]{:S(2)}) copy-start(bf16[3,64,3,128]{3,1,2,0:T(8,128)(2,1)} %copy-done.13) | copy-start | bytes 442372
  160.3 2.8 %copy-start.20 = (bf16[1,128,576]{1,2,0:T(8,128)(2,1)S(1)}, bf16[1,128,576]{1,2,0:T(8,128)(2,1)}, u32[]{:S(2)}) copy-start(bf16[1,128,576]{1,2,0:T(8,128)(2,1)} %param.10) | copy-start | bytes 442372
  170.1 5.5 %copy-start.18 = (bf16[128,1536]{1,0:T(8,128)(2,1)S(1)}, bf16[128,1536]{1,0:T(8,128)(2,1)}, u32[]{:S(2)}) copy-start(bf16[128,1536]{1,0:T(8,128)(2,1)} %copy-done.17) | copy-start | bytes 1179652
  177.6 1.0 copy-start.2
  177.6 1.1 copy-start.30
  177.6 1.2 copy-start.31
  180.8 1.5 copy-start.6
  180.9 1.5 copy-start.19
